TPU v7x, 512 devices: a whole 4x4x16 slice. The times are simulated.
512 devices in a mesh: wide: 128 (over x_lo, y, z), narrow: 4 (over x_hi, core).
Axes of the slice: x: 4 (x_hi: 2, x_lo: 2; x = x_hi * 2 + x_lo), y: 4, z: 16, core: 2. Of those that a mesh axis runs over, the one named last changes fastest.
Arguments:
- raw_ints: bfloat16 [4, 640, 128, 2, 384], P('narrow', 'wide'), may hold values from -5 to 5
- metric_root: bfloat16 [640, 640], P('wide'), may hold values from -0.25 to 0.25
- occ_energy: float32 [8, 2], replicated, may hold values from -1.6 to -0.4
- vir_energy: float32 [4, 384], replicated, may hold values from 0.3 to 2.5
- block_kpoint: int32 [4, 128], replicated, may hold values from 0 to 7
- occ_count: int32 [4, 128], replicated, may hold values from 1 to 2, as said below
Outputs:
- gamma: bfloat16 [4, 640, 128, 2, 384], P('narrow', None, 'wide')
- virt_density: float32 [147456], P(('wide', 'narrow'))
Inputs may be any that keep to these rules, and one draw needn't show every extreme that they name: `occ_count`: slot o of a block is live when o is less than its count; some block has all 2 slots live.
All inputs are finite; a program needn't handle non-finite values.
Results may differ from a plain program's by a relative error of at most 0.0043.
Values may be sent and summed in bfloat16 or wider, within the bound.
A program may use at most 64 MiB of HBM per device.

v0:
```python
import jax
import jax.numpy as jnp
from jax import lax
from jax.sharding import Mesh
from jax.sharding import PartitionSpec as P

WINDOW = 3
WIDE = ("wide_0", "wide_1", "wide_2")
NARROW = ("narrow_0", "narrow_1")
WIDE_NARROW = ("wide_0", "wide_1", "wide_2", "narrow_0", "narrow_1")


def in_order(parts, dim):
    parts = jnp.moveaxis(parts, 0, dim)
    dims = parts.shape
    return parts.reshape(*dims[:dim], dims[dim] * dims[dim + 1], *dims[dim + 2 :])


def gather_in_order(array, axes, order):
    parts = array
    for k in order:
        parts = lax.all_gather(parts, axes[k])
    done = order[::-1]
    back = [done.index(k) for k in range(len(axes))]
    parts = parts.transpose(*back, *range(len(axes), parts.ndim))
    return parts.reshape(-1, *array.shape)


def gather_axes(array, axes, order, dim):
    return in_order(gather_in_order(array, axes, order), dim)


def from_behind(value, axis, steps):
    count = lax.axis_size(axis)
    pairs = [(source, (source + steps) % count) for source in range(count)]
    return lax.ppermute(value, axis, pairs)


def partner(value, axis, bit):
    mask = 2**bit
    pairs = [(source, source ^ mask) for source in range(lax.axis_size(axis))]
    return lax.ppermute(value, axis, pairs)


def cut_along(array, dim, peers):
    before, after = (array.shape[:dim], array.shape[dim + 1 :])
    return jnp.moveaxis(array.reshape(*before, peers, -1, *after), dim, 0)


def scatter_pairs(array, chips, core, dim):
    sizes = (lax.axis_size(chips), lax.axis_size(core))
    parts = cut_along(array, dim, sizes[0] * sizes[1])
    inside = parts.shape[1:]
    parts = parts.reshape(*sizes, *inside).swapaxes(0, 1).reshape(-1, *inside)
    parts = lax.psum_scatter(parts, core, scatter_dimension=0, tiled=True)
    return lax.psum_scatter(parts, chips, scatter_dimension=0, tiled=True)[0]


def shards(raw_ints, metric_root, occ_energy, vir_energy, block_kpoint, occ_count):
    occ_slots = raw_ints.shape[3]
    vir_count = raw_ints.shape[4]
    row_width = occ_slots * vir_count
    wide_count = lax.axis_size(WIDE)
    group_count = lax.axis_size(NARROW)
    my_block = lax.axis_index(WIDE)
    my_group = lax.axis_index(NARROW)
    partner_group = (my_group + group_count // 2) % group_count
    flip_bit = group_count.bit_length() - 2
    regrouped = lax.all_to_all(raw_ints, WIDE, split_axis=2, concat_axis=1, tiled=True)
    aux_count = regrouped.shape[1]
    aux_rows = regrouped.reshape(aux_count, row_width)
    fitted = lax.dot_general(
        gather_axes(metric_root, WIDE, (0, 1, 2), 0),
        aux_rows,
        (((0,), (0,)), ((), ())),
        preferred_element_type=jnp.float32,
    ).astype(jnp.bfloat16)

    def window_blocks(source):
        shifted = [from_behind(source, WIDE, -offset) for offset in range(1, WINDOW)]
        return shifted

    paired = [
        partner(own_piece, NARROW, flip_bit) for own_piece in [fitted] + window_blocks(fitted)
    ]

    def block_state(group_index, block_index):
        k_point = lax.dynamic_slice(block_kpoint, (group_index, block_index), (1, 1))[0, 0]
        picked = jnp.sum(
            jnp.where(jnp.arange(occ_energy.shape[0])[:, None] == k_point, occ_energy, 0.0), axis=0
        )
        live_count = lax.dynamic_slice(occ_count, (group_index, block_index), (1, 1))[0, 0]
        live_slots = (jnp.arange(occ_slots) < live_count).astype(jnp.float32)
        return (picked, live_slots)

    vir_own = lax.dynamic_index_in_dim(vir_energy, my_group, 0, keepdims=False)
    vir_partner = lax.dynamic_index_in_dim(vir_energy, partner_group, 0, keepdims=False)
    occ_own, live_own = block_state(my_group, my_block)
    gamma_sum = jnp.zeros((aux_count, row_width), jnp.float32)
    density = jnp.zeros((vir_count, vir_count), jnp.float32)
    for offset in range(WINDOW):
        far_rows = paired[offset]
        occ_other, live_other = block_state(partner_group, (my_block + offset) % wide_count)
        coulomb = lax.dot_general(
            fitted, far_rows, (((0,), (0,)), ((), ())), preferred_element_type=jnp.float32
        )
        coulomb = coulomb.reshape(occ_slots, vir_count, occ_slots, vir_count)
        denominator = (
            occ_own[:, None, None, None]
            + occ_other[None, None, :, None]
            - vir_own[None, :, None, None]
            - vir_partner[None, None, None, :]
        )
        amplitude = (
            coulomb / denominator * live_own[:, None, None, None] * live_other[None, None, :, None]
        )
        mixed_amp = 2.0 * amplitude - jnp.transpose(amplitude, (0, 3, 2, 1))
        amp_half = amplitude.astype(jnp.bfloat16)
        mixed_half = mixed_amp.astype(jnp.bfloat16)
        gamma_sum = gamma_sum + lax.dot_general(
            far_rows,
            mixed_half.reshape(row_width, row_width),
            (((1,), (1,)), ((), ())),
            preferred_element_type=jnp.float32,
        )
        density = density + jnp.einsum(
            "iajc,ibjc->ab", mixed_half, amp_half, preferred_element_type=jnp.float32
        )
    norm_scale = 1.0 / (group_count * wide_count * vir_count)
    virt_density = (
        scatter_pairs(
            density.reshape(-1), ("wide_0", "wide_1", "wide_2", "narrow_0"), "narrow_1", 0
        )
        * norm_scale
    )
    return (
        gamma_sum.astype(jnp.bfloat16).reshape(1, aux_count, 1, occ_slots, vir_count),
        virt_density,
    )


def solution(mesh):
    torus = Mesh(
        mesh.devices.reshape(2, 4, 16, 2, 2), ("wide_0", "wide_1", "wide_2", "narrow_0", "narrow_1")
    )
    placed = (P(NARROW, WIDE, None, None, None), P(WIDE, None), P(), P(), P(), P())
    return jax.shard_map(
        shards,
        mesh=torus,
        in_specs=placed,
        out_specs=(P(NARROW, None, WIDE, None, None), P(WIDE_NARROW)),
        check_vma=False,
    )
```

profile of v0, /device:TPU:1, one launch (start us, length us, event | category | flops | bytes accessed | tf_op | source)
XLA Modules:
  0.0 660.8 jit_solution(11418079162293912562)
XLA Ops:
  7.2 2.8 copy.87
  10.0 21.4 %all-to-all-start = ((bf16[1,5,128,2,384]{4,3,1,0,2:T(2,128)(2,1)}), bf16[1,5,128,2,384]{4,3,1,0,2:T(2,128)(2,1)S(1)}, u32[]{:S(2)}, u32[]{:S(2)}) async-start(bf16[1,5,128,2,384]{4,3,1,0,2:T(2,128)(2,1)} %copy.87), calls=%async_computation | async-start | bytes 1966080 | tf_op jit(solution)/shard_map/all_to_all | solution.py:69
  31.5 3.5 all-gather.3
  35.0 9.9 %all-gather.1 = bf16[8,5,640]{2,1,0:T(8,128)(2,1)S(1)} all-gather(bf16[2,5,640]{2,1,0:T(8,128)(2,1)S(1)} %all-gather.3), channel_id=3, replica_groups=mesh['wide_0'=2,'wide_1'=4,'wide_2'=16,'narrow_0'=2,'narrow_1'=2] {'wide..., dimensions={0}, use_global_device_ids=true | all-gather | bytes 64000 | tf_op jit(solution)/shard_map/all_gather | solution.py:22
  45.0 52.5 %all-gather.2 = bf16[64,2,5,640]{3,1,2,0:T(2,128)(2,1)S(1)} all-gather(bf16[4,2,5,640]{3,1,2,0:T(2,128)(2,1)S(1)} %copy.85), channel_id=4, replica_groups=mesh['wide_0'=2,'wide_1'=4,'wide_2'=16,'narrow_0'=2,'narrow_1'=2] {'wide..., dimensions={0}, use_global_device_ids=true | all-gather | bytes 870400 | tf_op jit(solution)/shard_map/all_gather | solution.py:22
  99.2 5.9 collective-permute-start.1
  107.1 4.2 collective-permute-start.3
  113.1 4.4 collective-permute-start
  120.1 4.3 collective-permute-start.2
  125.7 33.9 %collective-permute-done.3 = bf16[640,768]{1,0:T(8,128)(2,1)} collective-permute-done((bf16[640,768]{1,0:T(8,128)(2,1)S(1)}, bf16[640,768]{1,0:T(8,128)(2,1)}, u32[]{:S(2)}, u32[]{:S(2)}) %collective-permute-start.3) | collective-permute-done | bytes 983072 | tf_op jit(solution)/shard_map/ppermute | solution.py:36
  159.6 4.6 collective-permute-start.4
  176.9 2.7 fusion.21
  181.9 5.7 fusion.4
  187.6 3.1 copy.93
  190.7 2.8 fusion.1
  195.4 3.1 copy.97
  198.5 2.8 fusion
  216.7 2.8 copy.99
  219.6 2.8 copy.95
  222.4 2.8 copy.91
  227.1 3.5 fusion.20
  232.9 27.7 %reduce-scatter.3.cloned.1.call-done = f32[256,288]{0,1:T(8,128)} async-done(((f32[512,288]{0,1:T(8,128)}), f32[256,288]{0,1:T(8,128)}) %reduce-scatter.3.cloned.1.call-update) | async-done | bytes 294928 | tf_op jit(solution)/shard_map/reduce_scatter | solution.py:55
  260.6 3.1 add_convert_fusion
  264.9 386.7 %all-reduce.3.cloned.1.call-done = f32[256,288]{0,1:T(8,128)} async-done(((f32[256,288]{0,1:T(8,128)}), f32[256,288]{0,1:T(8,128)}) %all-reduce.3.cloned.1.call-update) | async-done | bytes 294928
  (89 shorter events, 49.4 us)
Async XLA Ops:
  7.2 24.3 %copy-start.13 = (bf16[5,640]{1,0:T(8,128)(2,1)S(1)}, bf16[5,640]{1,0:T(8,128)(2,1)}, u32[]{:S(2)}) copy-start(bf16[5,640]{1,0:T(8,128)(2,1)} %param.7) | copy-start | bytes 19204
  10.0 88.0 %all-to-all-start = ((bf16[1,5,128,2,384]{4,3,1,0,2:T(2,128)(2,1)}), bf16[1,5,128,2,384]{4,3,1,0,2:T(2,128)(2,1)S(1)}, u32[]{:S(2)}, u32[]{:S(2)}) async-start(bf16[1,5,128,2,384]{4,3,1,0,2:T(2,128)(2,1)} %copy.87), calls=%async_computation | async-start | bytes 1966080 | tf_op jit(solution)/shard_map/all_to_all | solution.py:69
  31.4 229.2 %reduce-scatter.3.cloned.1.call-start = ((), (), s32[]{:S(2)}) async-start(), calls=%async_computation.2 | async-start | bytes 884736 | tf_op jit(solution)/shard_map/reduce_scatter | solution.py:55
  98.2 7.0 %copy-start.16 = (f32[4,384]{1,0:T(4,128)S(1)}, f32[4,384]{1,0:T(4,128)}, u32[]{:S(2)}) copy-start(f32[4,384]{1,0:T(4,128)} %param.9) | copy-start | bytes 18436
  98.2 7.6 %copy-start.14 = (s32[4,128]{1,0:T(4,128)S(1)}, s32[4,128]{1,0:T(4,128)}, u32[]{:S(2)}) copy-start(s32[4,128]{1,0:T(4,128)} %param.11) | copy-start | bytes 6148
  98.2 7.6 %copy-start.15 = (s32[4,128]{1,0:T(4,128)S(1)}, s32[4,128]{1,0:T(4,128)}, u32[]{:S(2)}) copy-start(s32[4,128]{1,0:T(4,128)} %param.10) | copy-start | bytes 6148
  98.2 21.7 %copy-start.17 = (f32[8,2]{0,1:T(2,128)S(1)}, f32[8,2]{0,1:T(2,128)}, u32[]{:S(2)}) copy-start(f32[8,2]{0,1:T(2,128)} %param.8) | copy-start | bytes 196
  99.2 66.7 %copy-start.18 = (bf16[640,768]{1,0:T(8,128)(2,1)}, bf16[640,768]{1,0:T(8,128)(2,1)S(1)}, u32[]{:S(2)}) copy-start(bf16[640,768]{1,0:T(8,128)(2,1)S(1)} %convolution_convert_fusion) | copy-start | bytes 2949124
  99.2 20.9 %collective-permute-start.1 = (bf16[640,768]{1,0:T(8,128)(2,1)S(1)}, bf16[640,768]{1,0:T(8,128)(2,1)}, u32[]{:S(2)}, u32[]{:S(2)}) collective-permute-start(bf16[640,768]{1,0:T(8,128)(2,1)S(1)} %convolution_convert_fusion), channel_id=1, source_target_pairs={{0,508},{4,0},{8,4},{12,8},{16,12},{20,16},{24,20},{28,24},{32,28}... | collective-permute-start | bytes 2949128 | tf_op jit(solution)/shard_map/ppermute | solution.py:36
  107.1 52.5 %collective-permute-start.3 = (bf16[640,768]{1,0:T(8,128)(2,1)S(1)}, bf16[640,768]{1,0:T(8,128)(2,1)}, u32[]{:S(2)}, u32[]{:S(2)}) collective-permute-start(bf16[640,768]{1,0:T(8,128)(2,1)S(1)} %convolution_convert_fusion), channel_id=1, source_target_pairs={{0,504},{4,508},{8,0},{12,4},{16,8},{20,12},{24,16},{28,20},{32,24... | collective-permute-start | bytes 2949128 | tf_op jit(solution)/shard_map/ppermute | solution.py:36
  113.1 52.8 %collective-permute-start = (bf16[640,768]{1,0:T(8,128)(2,1)S(1)}, bf16[640,768]{1,0:T(8,128)(2,1)S(1)}, u32[]{:S(2)}, u32[]{:S(2)}) collective-permute-start(bf16[640,768]{1,0:T(8,128)(2,1)S(1)} %convolution_convert_fusion), channel_id=1, source_target_pairs={{0,2},{1,3},{2,0},{3,1},{4,6},{5,7},{6,4},{7,5},{8,10},{9,11},{10,... | collective-permute-start | bytes 2949128 | tf_op jit(solution)/shard_map/ppermute | solution.py:42
  120.1 51.5 %collective-permute-start.2 = (bf16[640,768]{1,0:T(8,128)(2,1)}, bf16[640,768]{1,0:T(8,128)(2,1)}, u32[]{:S(2)}, u32[]{:S(2)}) collective-permute-start(bf16[640,768]{1,0:T(8,128)(2,1)} %collective-permute-done.1), channel_id=1, source_target_pairs={{0,2},{1,3},{2,0},{3,1},{4,6},{5,7},{6,4},{7,5},{8,10},{9,11},{10,... | collective-permute-start | bytes 2949128 | tf_op jit(solution)/shard_map/ppermute | solution.py:42
  159.6 17.3 %collective-permute-start.4 = (bf16[640,768]{1,0:T(8,128)(2,1)}, bf16[640,768]{1,0:T(8,128)(2,1)S(1)}, u32[]{:S(2)}, u32[]{:S(2)}) collective-permute-start(bf16[640,768]{1,0:T(8,128)(2,1)} %collective-permute-done.3), channel_id=1, source_target_pairs={{0,2},{1,3},{2,0},{3,1},{4,6},{5,7},{6,4},{7,5},{8,10},{9,11},{10,... | collective-permute-start | bytes 2949128 | tf_op jit(solution)/shard_map/ppermute | solution.py:42
  176.9 2.7 copy-start.11
  190.7 3.1 copy-start.1
  198.5 3.1 copy-start
  205.2 3.1 copy-start.9
  205.2 3.1 copy-start.10
  209.9 6.8 %copy-start.3 = (bf16[2,384,2,384]{1,3,2,0:T(8,128)(2,1)S(1)}, bf16[2,384,2,384]{1,3,2,0:T(8,128)(2,1)}, u32[]{:S(2)}) copy-start(bf16[2,384,2,384]{1,3,2,0:T(8,128)(2,1)} %copy-done.2) | copy-start | bytes 3538948
  215.1 436.5 %all-reduce.3.cloned.1.call-start = ((), (), s32[]{:S(2)}) async-start(), calls=%async_computation.3 | async-start | bytes 589824
  216.7 5.7 copy-start.5
  219.6 5.7 copy-start.6
  227.1 3.6 copy-start.20
  230.7 30.0 %copy-start.12 = (bf16[640,768]{1,0:T(8,128)(2,1)S(1)}, bf16[640,768]{1,0:T(8,128)(2,1)}, u32[]{:S(2)}) copy-start(bf16[640,768]{1,0:T(8,128)(2,1)} %copy-done.11) | copy-start | bytes 2949124
  (5 other events, 6.5 us)
Sparse Core Ops, SparseCore 0:
  215.2 45.3 reduce-scatter.2
  266.0 385.5 all-reduce.2
where the time goes:
time: 671 us; the launch traced here: 661 us
  waiting for transfers between devices  449 us (67%)
  blocking collectives  65.9 us (10%)
  starting transfers between devices  45.1 us (7%)
  local copies, waits for them, and re-layouts  40.5 us (6%)
  other arithmetic  23.8 us (4%)
  matrix products  22.4 us (3%)
  between operations  14.4 us (2%)
    unnamed x3, waiting for transfers between devices  387 us
    all_gather x3, blocking collectives, gather_in_order(): parts = lax.all_gather(parts, axes[k])  65.9 us
    ppermute x2, waiting for transfers between devices, from_behind(): return lax.ppermute(value, axis, pairs)  33.9 us
    reduce_scatter x1, waiting for transfers between devices, scatter_pairs(): parts = lax.psum_scatter(parts, core, scatter_dimension=0, tiled=True)  27.7 us
    all_to_all x1, starting transfers between devices, shards(): lax.all_to_all(raw_ints, WIDE, split_axis=2, concat_axis=1, tiled=True)  21.4 us
  transfers between devices with their start and end apart: 8, of which 4 were waited for; matrix products, arithmetic and copies ran while one was open for 6% of the time, Pallas kernels for 0%

commit v1 on v0

--- a/solution.py
+++ b/solution.py
@@ -1,8 +1,159 @@
+import functools
+
 import jax
 import jax.numpy as jnp
 from jax import lax
+from jax.experimental import pallas as pl
+from jax.experimental.pallas import tpu as pltpu
 from jax.sharding import Mesh
 from jax.sharding import PartitionSpec as P
+
+MESH_ID = pl.DeviceIdType.MESH
+
+
+def coords(w, n):
+    x, y, z = split_wide(w)
+    return (x, y, z, n // 2, n % 2)
+
+
+def split_wide(w):
+    return w // 64, (w // 16) % 4, w % 16
+
+
+def join_wide(x, y, z):
+    return x * 64 + y * 16 + z
+
+
+def slot_of(w):
+    x, y, z = split_wide(w)
+    return x * 64 + y * 16 + (z % 2) * 8 + z // 2
+
+
+def peer_at(step, w):
+    x, y, z = split_wide(w)
+    turn, side = step // 8, step % 8
+    half = (turn + 1) // 2
+    dz = jnp.where(turn % 2 == 1, half, 16 - half)
+    return join_wide((x + side // 4) % 2, (y + side % 4) % 4, (z + dz) % 16)
+
+
+def regroup_kernel(raw, root, recv, metric, ssem, rsem, msend, mrecv):
+    w = lax.axis_index(WIDE)
+    n = lax.axis_index(NARROW)
+    core = n % 2
+    sibling = n + 1 - 2 * core
+    x, y, z = split_wide(w)
+    barrier = pltpu.get_barrier_semaphore()
+
+    def greet(step, carry):
+        pl.semaphore_signal(barrier, inc=1, device_id=coords((w + step) % 128, n), device_id_type=MESH_ID)
+        return carry
+
+    lax.fori_loop(1, 128, greet, 0)
+    pl.semaphore_signal(barrier, inc=1, device_id=coords(w, sibling), device_id_type=MESH_ID)
+    pl.semaphore_wait(barrier, 128)
+
+    mine = slot_of(w)
+    par = (z + core) % 2
+
+    def send_metric(step, carry):
+        dz = 2 * step + core
+
+        @pl.when(dz != 0)
+        def _():
+            pltpu.make_async_remote_copy(
+                root, metric.at[mine], msend.at[0], mrecv.at[0],
+                device_id=coords(join_wide(x, y, (z + dz) % 16), n), device_id_type=MESH_ID,
+            ).start()
+
+        @pl.when(dz == 0)
+        def _():
+            pltpu.make_async_copy(root, metric.at[mine], mrecv.at[0]).start()
+
+        return carry
+
+    lax.fori_loop(0, 8, send_metric, 0)
+    pltpu.make_async_copy(raw.at[0, :, w], recv.at[mine], rsem).start()
+
+    def send_raw(step, carry):
+        peer = peer_at(step, w)
+
+        @pl.when(peer != w)
+        def _():
+            pltpu.make_async_remote_copy(
+                raw.at[0, :, peer], recv.at[mine], ssem, rsem, device_id=coords(peer, n), device_id_type=MESH_ID
+            ).start()
+
+        return carry
+
+    lax.fori_loop(0, 128, send_raw, 0)
+
+    line = metric.at[pl.ds(pl.multiple_of(x * 64 + y * 16 + par * 8, 8), 8)]
+    pltpu.make_async_copy(line, line, mrecv.at[0]).wait()
+    for step in range(1, 4):
+        pltpu.make_async_remote_copy(
+            line, line, msend.at[1], mrecv.at[1],
+            device_id=coords(join_wide(x, (y + step) % 4, z), n), device_id_type=MESH_ID,
+        ).start()
+    three = metric.at[pl.ds(0, 24)]
+    pltpu.make_async_copy(three, three, mrecv.at[1]).wait()
+    copies = []
+    for row in range(4):
+        part = metric.at[pl.ds(pl.multiple_of(x * 64 + row * 16 + par * 8, 8), 8)]
+        copies.append(pltpu.make_async_remote_copy(
+            part, part, msend.at[2], mrecv.at[2],
+            device_id=coords(join_wide(1 - x, y, z), n), device_id_type=MESH_ID,
+        ))
+    for copy in copies:
+        copy.start()
+    four = metric.at[pl.ds(0, 32)]
+    pltpu.make_async_copy(four, four, mrecv.at[2]).wait()
+    for row in range(8):
+        part = metric.at[pl.ds(pl.multiple_of(row * 16 + par * 8, 8), 8)]
+        pltpu.make_async_remote_copy(
+            part, part, msend.at[3], mrecv.at[3], device_id=coords(w, sibling), device_id_type=MESH_ID
+        ).start()
+    eight = metric.at[pl.ds(0, 64)]
+    pltpu.make_async_copy(eight, eight, mrecv.at[3]).wait()
+
+    @pl.when(core == 0)
+    def _():
+        part = metric.at[pl.ds(0, 7)]
+        pltpu.make_async_copy(part, part, msend.at[0]).wait()
+
+    @pl.when(core == 1)
+    def _():
+        part = metric.at[pl.ds(0, 8)]
+        pltpu.make_async_copy(part, part, msend.at[0]).wait()
+
+    pltpu.make_async_copy(three, three, msend.at[1]).wait()
+    pltpu.make_async_copy(four, four, msend.at[2]).wait()
+    pltpu.make_async_copy(eight, eight, msend.at[3]).wait()
+    others = recv.at[pl.ds(0, 127)]
+    pltpu.make_async_copy(others, others, ssem).wait()
+    pltpu.make_async_copy(recv, recv, rsem).wait()
+
+
+def regroup(raw_ints, metric_root):
+    rows, cols = metric_root.shape
+    return pl.pallas_call(
+        regroup_kernel,
+        name="regroup",
+        out_shape=(
+            jax.ShapeDtypeStruct((128,) + raw_ints.shape[1:2] + raw_ints.shape[3:], jnp.bfloat16),
+            jax.ShapeDtypeStruct((128, rows, cols), jnp.bfloat16),
+        ),
+        in_specs=[pl.BlockSpec(memory_space=pltpu.VMEM)] * 2,
+        out_specs=(pl.BlockSpec(memory_space=pltpu.VMEM),) * 2,
+        scratch_shapes=[
+            pltpu.SemaphoreType.DMA,
+            pltpu.SemaphoreType.DMA,
+            pltpu.SemaphoreType.DMA((4,)),
+            pltpu.SemaphoreType.DMA((4,)),
+        ],
+        compiler_params=pltpu.CompilerParams(collective_id=0, has_side_effects=True),
+    )(raw_ints, metric_root)
+
 
 WINDOW = 3
 WIDE = ("wide_0", "wide_1", "wide_2")
@@ -66,12 +217,11 @@
     my_group = lax.axis_index(NARROW)
     partner_group = (my_group + group_count // 2) % group_count
     flip_bit = group_count.bit_length() - 2
-    regrouped = lax.all_to_all(raw_ints, WIDE, split_axis=2, concat_axis=1, tiled=True)
-    aux_count = regrouped.shape[1]
-    aux_rows = regrouped.reshape(aux_count, row_width)
+    blocks, roots = regroup(raw_ints, metric_root)
+    aux_count = wide_count * metric_root.shape[0]
     fitted = lax.dot_general(
-        gather_axes(metric_root, WIDE, (0, 1, 2), 0),
-        aux_rows,
+        roots.reshape(aux_count, aux_count),
+        blocks.reshape(aux_count, row_width),
         (((0,), (0,)), ((), ())),
         preferred_element_type=jnp.float32,
     ).astype(jnp.bfloat16)

time: 671 us -> 656 us (0.978)
  blocking collectives: 65.9 us -> 0 us
  Pallas kernels: 0 us -> 65.5 us
  starting transfers between devices: 45.1 us -> 31.1 us
    all_gather x3 -> x0, blocking collectives: 65.9 us -> none  [gather_in_order(): parts = lax.all_gather(parts, axes[k])]
    pallas_call x0 -> x1, Pallas kernels: none -> 65.5 us  [regroup(): pl.pallas_call(regroup_kernel, name='regroup', out_shape=(jax.ShapeDtypeS...]
    all_to_all x1 -> x0, starting transfers between devices: 21.4 us -> none  [shards(): lax.all_to_all(raw_ints, WIDE, split_axis=2, concat_axis=1, tiled=True)]
    reduce_scatter x1, waiting for transfers between devices: 27.7 us -> 10.3 us  [scatter_pairs(): parts = lax.psum_scatter(parts, core, scatter_dimension=0, tiled=True)]
    ppermute x2, waiting for transfers between devices: 33.9 us -> 43.6 us  [from_behind(): return lax.ppermute(value, axis, pairs)]
    ppermute x3, waiting for transfers between devices: 0.37 us -> 8.67 us  [partner(): return lax.ppermute(value, axis, pairs)]
  transfers between devices with their start and end apart: 8 -> 7, of which waited for: 4 -> 5; matrix products, arithmetic and copies ran while one was open for 6% -> 6% of each run, Pallas kernels for 0% -> 0%
where the time goes in v1:
time: 656 us; the launch traced here: 646 us
  waiting for transfers between devices  449 us (68%)
  Pallas kernels  65.5 us (10%)
  local copies, waits for them, and re-layouts  38 us (6%)
  starting transfers between devices  31.1 us (5%)
  matrix products  23.9 us (4%)
  other arithmetic  23.8 us (4%)
  between operations  14.4 us (2%)
    unnamed x3, waiting for transfers between devices  387 us
    pallas_call x1, Pallas kernels, regroup(): pl.pallas_call(regroup_kernel, name='regroup', out_shape=(jax.ShapeDtypeS...  65.5 us
    ppermute x2, waiting for transfers between devices, from_behind(): return lax.ppermute(value, axis, pairs)  43.6 us
    ppermute x2, starting transfers between devices, from_behind(): return lax.ppermute(value, axis, pairs)  16.6 us
    ppermute x3, starting transfers between devices, partner(): return lax.ppermute(value, axis, pairs)  14.3 us
  transfers between devices with their start and end apart: 7, of which 5 were waited for; matrix products, arithmetic and copies ran while one was open for 6% of the time, Pallas kernels for 0%

profile of v1, /device:TPU:1, one launch (start us, length us, event | category | flops | bytes accessed | tf_op | source)
XLA Modules:
  0.0 645.9 jit_solution(16638434098577473250)
XLA Ops:
  7.2 65.5 %regroup.1 = (bf16[128,5,2,384]{3,2,1,0:T(2,128)(2,1)}, bf16[128,5,640]{2,1,0:T(8,128)(2,1)}) custom-call(bf16[1,5,128,2,384]{4,3,2,1,0:T(2,128)(2,1)} %raw.1, bf16[5,640]{1,0:T(8,128)(2,1)} %root.1), custom_call_target="tpu_custom_call" | custom-call | tf_op jit(solution)/shard_map/regroup/pallas_call | solution.py:139
  75.7 14.6 %collective-permute-start.1 = (bf16[640,768]{1,0:T(8,128)(2,1)S(1)}, bf16[640,768]{1,0:T(8,128)(2,1)}, u32[]{:S(2)}, u32[]{:S(2)}) collective-permute-start(bf16[640,768]{1,0:T(8,128)(2,1)S(1)} %convolution_convert_fusion), channel_id=1, source_target_pairs={{0,508},{4,0},{8,4},{12,8},{16,12},{20,16},{24,20},{28,24},{32,28}... | collective-permute-start | bytes 2949128 | tf_op jit(solution)/shard_map/ppermute | solution.py:187
  90.4 4.7 collective-permute-start
  103.3 13.2 %collective-permute-done.1 = bf16[640,768]{1,0:T(8,128)(2,1)} collective-permute-done((bf16[640,768]{1,0:T(8,128)(2,1)S(1)}, bf16[640,768]{1,0:T(8,128)(2,1)}, u32[]{:S(2)}, u32[]{:S(2)}) %collective-permute-start.1) | collective-permute-done | bytes 983072 | tf_op jit(solution)/shard_map/ppermute | solution.py:187
  116.5 4.8 collective-permute-start.2
  122.5 30.5 %collective-permute-done.3 = bf16[640,768]{1,0:T(8,128)(2,1)} collective-permute-done((bf16[640,768]{1,0:T(8,128)(2,1)S(1)}, bf16[640,768]{1,0:T(8,128)(2,1)}, u32[]{:S(2)}, u32[]{:S(2)}) %collective-permute-start.3) | collective-permute-done | bytes 983072 | tf_op jit(solution)/shard_map/ppermute | solution.py:187
  153.0 4.8 collective-permute-start.4
  159.8 2.6 fusion.17
  164.8 2.6 fusion.19
  169.7 8.7 %collective-permute-done.4 = bf16[640,768]{1,0:T(8,128)(2,1)S(1)} collective-permute-done((bf16[640,768]{1,0:T(8,128)(2,1)}, bf16[640,768]{1,0:T(8,128)(2,1)S(1)}, u32[]{:S(2)}, u32[]{:S(2)}) %collective-permute-start.4) | collective-permute-done | bytes 983072 | tf_op jit(solution)/shard_map/ppermute | solution.py:193
  178.4 2.7 fusion.21
  183.4 5.7 fusion.4
  189.1 3.1 copy.80
  192.2 2.8 fusion.1
  197.0 3.1 copy.84
  200.0 2.8 fusion
  218.2 2.9 copy.86
  221.0 2.8 copy.82
  223.9 2.8 copy.78
  228.6 3.5 fusion.20
  232.1 3.5 fusion.18
  235.6 10.3 %reduce-scatter.3.cloned.1.call-done = f32[256,288]{0,1:T(8,128)} async-done(((f32[512,288]{0,1:T(8,128)}), f32[256,288]{0,1:T(8,128)}) %reduce-scatter.3.cloned.1.call-update) | async-done | bytes 294928 | tf_op jit(solution)/shard_map/reduce_scatter | solution.py:206
  245.9 3.1 add_convert_fusion
  250.1 386.6 %all-reduce.3.cloned.1.call-done = f32[256,288]{0,1:T(8,128)} async-done(((f32[256,288]{0,1:T(8,128)}), f32[256,288]{0,1:T(8,128)}) %all-reduce.3.cloned.1.call-update) | async-done | bytes 294928
  (78 shorter events, 44.0 us)
Async XLA Ops:
  7.2 238.7 %reduce-scatter.3.cloned.1.call-start = ((), (), s32[]{:S(2)}) async-start(), calls=%async_computation.1 | async-start | bytes 884736 | tf_op jit(solution)/shard_map/reduce_scatter | solution.py:206
  72.7 1.6 copy-start.11
  74.7 22.3 %copy-start.16 = (f32[4,384]{1,0:T(4,128)S(1)}, f32[4,384]{1,0:T(4,128)}, u32[]{:S(2)}) copy-start(f32[4,384]{1,0:T(4,128)} %param.9) | copy-start | bytes 18436
  74.7 22.9 %copy-start.14 = (s32[4,128]{1,0:T(4,128)S(1)}, s32[4,128]{1,0:T(4,128)}, u32[]{:S(2)}) copy-start(s32[4,128]{1,0:T(4,128)} %param.11) | copy-start | bytes 6148
  74.7 22.9 %copy-start.15 = (s32[4,128]{1,0:T(4,128)S(1)}, s32[4,128]{1,0:T(4,128)}, u32[]{:S(2)}) copy-start(s32[4,128]{1,0:T(4,128)} %param.10) | copy-start | bytes 6148
  74.7 28.4 %copy-start.17 = (f32[8,2]{0,1:T(2,128)S(1)}, f32[8,2]{0,1:T(2,128)}, u32[]{:S(2)}) copy-start(f32[8,2]{0,1:T(2,128)} %param.8) | copy-start | bytes 196
  75.7 84.0 %copy-start.18 = (bf16[640,768]{1,0:T(8,128)(2,1)}, bf16[640,768]{1,0:T(8,128)(2,1)S(1)}, u32[]{:S(2)}) copy-start(bf16[640,768]{1,0:T(8,128)(2,1)S(1)} %convolution_convert_fusion) | copy-start | bytes 2949124
  75.7 40.7 %collective-permute-start.1 = (bf16[640,768]{1,0:T(8,128)(2,1)S(1)}, bf16[640,768]{1,0:T(8,128)(2,1)}, u32[]{:S(2)}, u32[]{:S(2)}) collective-permute-start(bf16[640,768]{1,0:T(8,128)(2,1)S(1)} %convolution_convert_fusion), channel_id=1, source_target_pairs={{0,508},{4,0},{8,4},{12,8},{16,12},{20,16},{24,20},{28,24},{32,28}... | collective-permute-start | bytes 2949128 | tf_op jit(solution)/shard_map/ppermute | solution.py:187
  90.4 69.4 %collective-permute-start = (bf16[640,768]{1,0:T(8,128)(2,1)S(1)}, bf16[640,768]{1,0:T(8,128)(2,1)}, u32[]{:S(2)}, u32[]{:S(2)}) collective-permute-start(bf16[640,768]{1,0:T(8,128)(2,1)S(1)} %convolution_convert_fusion), channel_id=1, source_target_pairs={{0,2},{1,3},{2,0},{3,1},{4,6},{5,7},{6,4},{7,5},{8,10},{9,11},{10,... | collective-permute-start | bytes 2949128 | tf_op jit(solution)/shard_map/ppermute | solution.py:193
  95.1 57.9 %collective-permute-start.3 = (bf16[640,768]{1,0:T(8,128)(2,1)S(1)}, bf16[640,768]{1,0:T(8,128)(2,1)}, u32[]{:S(2)}, u32[]{:S(2)}) collective-permute-start(bf16[640,768]{1,0:T(8,128)(2,1)S(1)} %convolution_convert_fusion), channel_id=1, source_target_pairs={{0,504},{4,508},{8,0},{12,4},{16,8},{20,12},{24,16},{28,20},{32,24... | collective-permute-start | bytes 2949128 | tf_op jit(solution)/shard_map/ppermute | solution.py:187
  116.5 48.3 %collective-permute-start.2 = (bf16[640,768]{1,0:T(8,128)(2,1)}, bf16[640,768]{1,0:T(8,128)(2,1)}, u32[]{:S(2)}, u32[]{:S(2)}) collective-permute-start(bf16[640,768]{1,0:T(8,128)(2,1)} %collective-permute-done.1), channel_id=1, source_target_pairs={{0,2},{1,3},{2,0},{3,1},{4,6},{5,7},{6,4},{7,5},{8,10},{9,11},{10,... | collective-permute-start | bytes 2949128 | tf_op jit(solution)/shard_map/ppermute | solution.py:193
  153.0 25.4 %collective-permute-start.4 = (bf16[640,768]{1,0:T(8,128)(2,1)}, bf16[640,768]{1,0:T(8,128)(2,1)S(1)}, u32[]{:S(2)}, u32[]{:S(2)}) collective-permute-start(bf16[640,768]{1,0:T(8,128)(2,1)} %collective-permute-done.3), channel_id=1, source_target_pairs={{0,2},{1,3},{2,0},{3,1},{4,6},{5,7},{6,4},{7,5},{8,10},{9,11},{10,... | collective-permute-start | bytes 2949128 | tf_op jit(solution)/shard_map/ppermute | solution.py:193
  178.4 2.7 copy-start.12
  192.2 3.1 copy-start.1
  200.0 3.1 copy-start
  203.1 1.6 copy-start.2
  206.7 3.1 copy-start.9
  206.7 3.1 copy-start.10
  211.4 6.7 %copy-start.3 = (bf16[2,384,2,384]{1,3,2,0:T(8,128)(2,1)S(1)}, bf16[2,384,2,384]{1,3,2,0:T(8,128)(2,1)}, u32[]{:S(2)}) copy-start(bf16[2,384,2,384]{1,3,2,0:T(8,128)(2,1)} %copy-done.2) | copy-start | bytes 3538948
  216.6 420.2 %all-reduce.3.cloned.1.call-start = ((), (), s32[]{:S(2)}) async-start(), calls=%async_computation.2 | async-start | bytes 589824
  218.2 5.7 copy-start.5
  221.0 5.7 copy-start.6
  226.7 1.6 copy-start.8
  232.0 13.8 %copy-start.13 = (bf16[640,768]{1,0:T(8,128)(2,1)S(1)}, bf16[640,768]{1,0:T(8,128)(2,1)}, u32[]{:S(2)}) copy-start(bf16[640,768]{1,0:T(8,128)(2,1)} %copy-done.12) | copy-start | bytes 2949124
  (2 other events, 2.3 us)
Sparse Core Ops, SparseCore 0:
  216.7 29.0 reduce-scatter.2
  251.2 385.4 all-reduce.2
